TPU v7x, 256 devices: a whole 4x4x8 slice. The times are simulated.
256 devices in a mesh: wide: 64 (over y, x, z_lo), narrow: 4 (over z_hi, core).
Axes of the slice: x: 4, y: 4, z: 8 (z_hi: 2, z_lo: 4; z = z_hi * 4 + z_lo), core: 2. Of those that a mesh axis runs over, the one named last changes fastest.
Arguments:
- volume: float32 [1024, 48, 1024], P('wide', None, 'narrow'), may hold values from 0 to 2
- codes_in: bfloat16 [1024, 72, 1536], P('wide', None, 'narrow'), may hold values from -4 to 4
- x_transform: float32 [1024, 1024], replicated, may hold values from -1 to 1, as said below
- y_atoms: bfloat16 [1024, 1536], replicated, may hold values from -0.1875 to 0.1875
- de_atoms: bfloat16 [48, 72], replicated, may hold values from -0.875 to 0.875
Outputs:
- codes_out: bfloat16 [1024, 72, 1536], P('wide', None, 'narrow')
- estimate: bfloat16 [1024, 48, 1024], P('wide', None, 'narrow')
Inputs may be any that keep to these rules, and one draw needn't show every extreme that they name: x_transform is orthonormal: its transpose is its inverse.
All inputs are finite; a program needn't handle non-finite values.
Results may differ from a plain program's by a relative error of at most 0.0065.
Values may be sent and summed in bfloat16 or wider, within the bound.
A program may use at most 64 MiB of HBM per device.

v0:
```python
import jax
import jax.numpy as jnp
from jax import lax
from jax.sharding import PartitionSpec as P

step_size = 0.06
threshold = 0.05
best = lax.Precision.HIGHEST


def shards(volume, codes_in, x_transform, y_atoms, de_atoms):
    xrows, depth, ylocal = volume.shape
    klocal = codes_in.shape[2]
    where = lax.axis_index("narrow")
    y_rows = lax.dynamic_slice_in_dim(y_atoms, where * ylocal, ylocal, 0)
    y_cols = lax.dynamic_slice_in_dim(y_atoms, where * klocal, klocal, 1)
    de_wide = de_atoms.astype(jnp.float32)

    def apply_x(columns, forward):
        if forward:
            return jnp.dot(x_transform, columns, precision=best)
        return lax.dot_general(x_transform, columns, (((0,), (0,)), ((), ())), precision=best)

    def along_x(field, forward):
        flat = field.reshape(xrows, depth * ylocal)
        columns = lax.all_to_all(flat, "wide", split_axis=1, concat_axis=0, tiled=True)
        mixed = apply_x(columns, forward)
        returned = lax.all_to_all(mixed, "wide", split_axis=0, concat_axis=1, tiled=True)
        return returned.reshape(xrows, depth, ylocal)

    def rebuild(codes):
        atoms = jnp.einsum(
            "fk,bkc->bfc", de_atoms, codes, preferred_element_type=jnp.float32
        ).astype(jnp.bfloat16)
        return jnp.einsum(
            "bfc,yc->bfy",
            lax.all_gather(atoms, "narrow", axis=2, tiled=True),
            y_rows,
            preferred_element_type=jnp.float32,
        )

    target = along_x(volume, True)
    codes = codes_in
    misfit = rebuild(codes) - target
    pulled = jnp.einsum("fk,bfy->bky", de_wide, misfit, precision=best).astype(jnp.bfloat16)
    grads = jnp.einsum(
        "bky,yc->bkc",
        lax.all_gather(pulled, "narrow", axis=2, tiled=True),
        y_cols,
        preferred_element_type=jnp.float32,
    )
    moved = codes.astype(jnp.float32) - step_size * grads
    codes = (moved - jnp.clip(moved, -threshold, threshold)).astype(jnp.bfloat16)
    image = rebuild(codes)
    estimate = jnp.maximum(along_x(image, False), 0.0).astype(jnp.bfloat16)
    return (codes, estimate)


def solution(mesh):
    return jax.shard_map(
        shards,
        mesh=mesh,
        in_specs=(P("wide", None, "narrow"), P("wide", None, "narrow"), P(), P(), P()),
        out_specs=(P("wide", None, "narrow"), P("wide", None, "narrow")),
        check_vma=False,
    )
```

profile of v0, /device:TPU:1, one launch (start us, length us, event | category | flops | bytes accessed | tf_op | source)
XLA Modules:
  0.0 301.2 jit_solution(1969324107720229944)
XLA Ops:
  7.2 0.0 copy-start
  7.2 0.0 all-gather.4.cloned.1.call-start
  7.2 2.5 fusion.2
  9.7 0.0 all-gather.4.cloned.1.call-update
  9.7 2.5 all_to_all.48
  12.2 0.0 copy-start.1
  12.2 2.0 copy.14
  14.2 66.0 %all_to_all.64 = f32[16,64,192]{2,0,1:T(8,128)S(1)} all-to-all(f32[16,64,192]{2,0,1:T(8,128)S(1)} %copy.14), channel_id=1, replica_groups=mesh['wide'=64,'narrow'=4] {'wide'}, dimensions={1} | all-to-all | bytes 1572864 | tf_op jit(solution)/shard_map/all_to_all | solution.py:26
  80.3 0.0 copy-done.1
  80.3 4.4 %fusion.18 = f32[64,16,192]{2,1,0:T(8,128)} fusion(f32[64,16,1024]{2,1,0:T(8,128)S(1)} %bitcast.46, f32[1024,192,1]{1,0,2:T(8,128)S(1)} %bitcast.47), kind=kOutput, calls=%fused_computation.25 | convolution fusion | flops 2415919104 | bytes 5767168 | tf_op jit(solution)/shard_map/dot_general | solution.py:21
  84.6 5.6 %all-to-all-start.1 = ((f32[64,16,192]{2,1,0:T(8,128)}), f32[64,16,192]{2,1,0:T(8,128)}, u32[]{:S(2)}, u32[]{:S(2)}) async-start(f32[64,16,192]{2,1,0:T(8,128)} %fusion.18), calls=%async_computation.1 | async-start | bytes 2097152 | tf_op jit(solution)/shard_map/all_to_all | solution.py:28
  90.3 0.0 all-gather.6.cloned.1.call-start
  90.3 28.1 %all-to-all-done.1 = f32[64,16,192]{2,1,0:T(8,128)} async-done(((f32[64,16,192]{2,1,0:T(8,128)}), f32[64,16,192]{2,1,0:T(8,128)}, u32[]{:S(2)}, u32[]{:S(2)}) %all-to-all-start.1) | async-done | bytes 786464 | tf_op jit(solution)/shard_map/all_to_all | solution.py:28
  118.5 2.8 copy.16
  121.3 2.7 reshape.30
  124.0 0.0 copy-start.4
  124.0 0.0 all-gather.4.cloned.1.call-done
  124.0 0.0 copy-done
  124.0 2.7 convolution_subtract_fusion
  126.7 0.0 copy-done.4
  126.7 1.5 fusion.1
  128.2 0.0 all-gather.6.cloned.1.call-update
  128.2 0.2 all-gather.8.cloned.1.call-start
  128.4 45.1 %all-gather.6.cloned.1.call-done = bf16[16,72,1024]{2,1,0:T(8,128)(2,1)} async-done(((bf16[16,72,256]{2,1,0:T(8,128)(2,1)}), bf16[16,72,1024]{2,1,0:T(8,128)(2,1)}) %all-gather.6.cloned.1.call-update) | async-done | bytes 2359312 | tf_op jit(solution)/shard_map/all_gather | solution.py:48
  173.5 3.3 %fusion = bf16[16,72,384]{2,1,0:T(8,128)(2,1)S(1)} fusion(bf16[16,72,384]{2,1,0:T(8,128)(2,1)} %param.6, bf16[16,72,1024]{2,1,0:T(8,128)(2,1)} %all-gather.6.cloned.1.call-done, bf16[1024,1536]{1,0:T(8,128)(2,1)S(1)} %copy-done, s32[]{:T(128)S(6)} %select_n.7), kind=kOutput, calls=%fused_computation.1 | convolution fusion | flops 908623872 | bytes 4915204 | tf_op jit(solution)/shard_map/bky,yc->bkc/dot_general | solution.py:46
  176.9 0.0 copy-start.3
  176.9 0.9 copy-done.3
  177.8 1.1 fusion.3
  179.0 0.0 all-gather.8.cloned.1.call-update
  179.0 42.3 %all-gather.8.cloned.1.call-done = bf16[16,48,1536]{2,1,0:T(8,128)(2,1)} async-done(((bf16[16,48,384]{2,1,0:T(8,128)(2,1)}), bf16[16,48,1536]{2,1,0:T(8,128)(2,1)}) %all-gather.8.cloned.1.call-update) | async-done | bytes 2359312 | tf_op jit(solution)/shard_map/all_gather | solution.py:37
  221.3 3.4 %fusion.5 = f32[16,48,256]{2,1,0:T(8,128)} fusion(bf16[16,48,1536]{2,1,0:T(8,128)(2,1)} %all-gather.8.cloned.1.call-done, bf16[1024,1536]{1,0:T(8,128)(2,1)S(1)} %copy-done, s32[]{:T(128)S(6)} %select_n.6), kind=kOutput, calls=%fused_computation.12 | convolution fusion | flops 603979776 | bytes 3932164 | tf_op jit(solution)/shard_map/bfc,yc->bfy/dot_general | solution.py:35
  224.7 2.5 all_to_all.54
  227.2 0.0 copy-start.2
  227.2 2.0 copy.17
  229.2 35.8 %all_to_all.65 = f32[16,64,192]{2,0,1:T(8,128)S(1)} all-to-all(f32[16,64,192]{2,0,1:T(8,128)S(1)} %copy.17), channel_id=1, replica_groups=mesh['wide'=64,'narrow'=4] {'wide'}, dimensions={1} | all-to-all | bytes 1572864 | tf_op jit(solution)/shard_map/all_to_all | solution.py:26
  265.0 0.0 copy-done.2
  265.0 3.0 convolution_bitcast_fusion
  268.0 1.0 copy.18
  269.0 22.1 %all_to_all.66 = bf16[64,16,192]{2,1,0:T(8,128)(2,1)S(1)} all-to-all(bf16[64,16,192]{2,1,0:T(8,128)(2,1)} %bitcast.49), channel_id=1, replica_groups=mesh['wide'=64,'narrow'=4] {'wide'}, dimensions={0} | all-to-all | bytes 786432 | tf_op jit(solution)/shard_map/all_to_all | solution.py:28
  291.1 0.1 fusion.11
  291.2 0.9 copy.19
  292.1 2.5 convert_element_type.44
Async XLA Ops:
  7.2 116.9 %copy-start = (bf16[1024,1536]{1,0:T(8,128)(2,1)S(1)}, bf16[1024,1536]{1,0:T(8,128)(2,1)}, u32[]{:S(2)}) copy-start(bf16[1024,1536]{1,0:T(8,128)(2,1)} %param.8) | copy-start | bytes 9437188
  7.2 116.8 %all-gather.4.cloned.1.call-start = ((), (), s32[]{:S(2)}) async-start(), calls=%async_computation.4 | async-start | bytes 2949120 | tf_op jit(solution)/shard_map/all_gather | solution.py:37
  12.2 68.0 %copy-start.1 = (f32[1024,1024]{1,0:T(8,128)S(1)}, f32[1024,1024]{1,0:T(8,128)}, u32[]{:S(2)}) copy-start(f32[1024,1024]{1,0:T(8,128)} %param.7) | copy-start | bytes 12582916
  84.6 33.8 %all-to-all-start.1 = ((f32[64,16,192]{2,1,0:T(8,128)}), f32[64,16,192]{2,1,0:T(8,128)}, u32[]{:S(2)}, u32[]{:S(2)}) async-start(f32[64,16,192]{2,1,0:T(8,128)} %fusion.18), calls=%async_computation.1 | async-start | bytes 2097152 | tf_op jit(solution)/shard_map/all_to_all | solution.py:28
  90.3 83.3 %all-gather.6.cloned.1.call-start = ((), (), s32[]{:S(2)}) async-start(), calls=%async_computation.5 | async-start | bytes 2949120 | tf_op jit(solution)/shard_map/all_gather | solution.py:48
  124.0 2.7 copy-start.4
  128.2 93.1 %all-gather.8.cloned.1.call-start = ((), (), s32[]{:S(2)}) async-start(), calls=%async_computation.6 | async-start | bytes 2949120 | tf_op jit(solution)/shard_map/all_gather | solution.py:37
  176.9 0.9 copy-start.3
  227.2 37.8 %copy-start.2 = (f32[1024,1024]{1,0:T(8,128)S(1)}, f32[1024,1024]{1,0:T(8,128)}, u32[]{:S(2)}) copy-start(f32[1024,1024]{1,0:T(8,128)} %param.7) | copy-start | bytes 12582916
Sparse Core Ops, SparseCore 0:
  9.8 60.9 all-gather.3
  128.3 45.1 all-gather.5
  179.1 42.1 all-gather.7
where the time goes:
time: 302 us; the launch traced here: 301 us
  blocking collectives  124 us (41%)
  waiting for transfers between devices  116 us (38%)
  matrix products  21.8 us (7%)
  local copies, waits for them, and re-layouts  19.9 us (7%)
  between operations  13.8 us (5%)
  starting transfers between devices  5.94 us (2%)
    all_to_all x2, blocking collectives, along_x(): lax.all_to_all(flat, 'wide', split_axis=1, concat_axis=0, tiled=True)  102 us
    all_gather x1, waiting for transfers between devices, shards(): lax.all_gather(pulled, 'narrow', axis=2, tiled=True)  45.1 us
    all_gather x2, waiting for transfers between devices, rebuild(): lax.all_gather(atoms, 'narrow', axis=2, tiled=True)  42.3 us
    all_to_all x1, waiting for transfers between devices, along_x(): lax.all_to_all(mixed, 'wide', split_axis=0, concat_axis=1, tiled=True)  28.1 us
    all_to_all x1, blocking collectives, along_x(): lax.all_to_all(mixed, 'wide', split_axis=0, concat_axis=1, tiled=True)  22.1 us
    all_to_all x4, local copies, waits for them, and re-layouts, along_x(): lax.all_to_all(flat, 'wide', split_axis=1, concat_axis=0, tiled=True)  8.96 us
  transfers between devices with their start and end apart: 4, of which 3 were waited for; matrix products, arithmetic and copies ran while one was open for 4% of the time, Pallas kernels for 0%

commit v1 on v0

v1 whole, which is shorter than its diff:
```python
import jax
import jax.numpy as jnp
from jax import lax
from jax.experimental import pallas as pl
from jax.experimental.pallas import tpu as pltpu
from jax.sharding import PartitionSpec as P

step_size = 0.06
threshold = 0.05
BF = jnp.bfloat16
F32 = jnp.float32
MESH = pl.DeviceIdType.MESH


def mm(a, b):
    return jnp.dot(a, b, preferred_element_type=F32)


def nt(a, b):
    return lax.dot_general(a, b, (((1,), (1,)), ((), ())), preferred_element_type=F32)


def tn(a, b):
    return lax.dot_general(a, b, (((0,), (0,)), ((), ())), preferred_element_type=F32)


def shrink(codes, grads):
    moved = codes - step_size * grads
    return (moved - jnp.clip(moved, -threshold, threshold)).astype(BF)


def remote(src, dst, send, recv, device):
    return pltpu.make_async_remote_copy(
        src_ref=src, dst_ref=dst, send_sem=send, recv_sem=recv, device_id=device, device_id_type=MESH
    )


def kernel(
    vol, codes, xin, din, de,
    new_codes, est,
    xv, xrows, xcols, dv, codes4, send1, recv1, send2, recv2, send3, recv3, send4, recv4, qsend, qrecv, atoms, fresh,
    xsem, dsem, ssem1, rsem1, fsem1, gsem1, ssem2, rsem2, ssem3, rsem3, fsem3, gsem3, ssem4, rsem4,
    csend, crecv, qssem, qrsem, lsem,
):
    w = lax.axis_index("wide")
    n = lax.axis_index("narrow")
    half = n // 2
    core = n % 2
    chip = 2 * w + half
    twin = (w, 2 * half + 1 - core)
    bit = lax.rem(w // 2, 2)

    load_x = pltpu.make_async_copy(xin, xv, xsem)
    load_d = pltpu.make_async_copy(din, dv, dsem)
    load_x.start()
    load_d.start()

    barrier = pltpu.get_barrier_semaphore()

    def greet_to(i, c):
        to = 4 * (i // 2) + 2 * core + lax.rem(i, 2)
        pl.semaphore_signal(barrier, inc=1, device_id=(to, 2 * half + 1 - bit), device_id_type=MESH)
        return c

    def greet_from(i, c):
        frm = 4 * (i // 2) + 2 * (1 - core) + lax.rem(i, 2)
        pl.semaphore_signal(barrier, inc=1, device_id=(frm, 2 * half + bit), device_id_type=MESH)
        return c

    for d in (1, 2, 3):
        pl.semaphore_signal(barrier, inc=1, device_id=(w, lax.rem(n + d, 4)), device_id_type=MESH)
    lax.fori_loop(0, 32, greet_to, 0)
    lax.fori_loop(0, 32, greet_from, 0)

    for f in range(48):
        rows = vol[:, f, :].astype(BF)
        for b in range(2):
            send1[f // 3, b, f % 3] = rows[:, 128 * b : 128 * b + 128]

    pl.semaphore_wait(barrier, 67)

    def start1(i, c):
        t = lax.rem(w // 4 + i // 2, 16)
        b = lax.rem(w + i, 2)
        remote(
            send1.at[t, b], recv1.at[w // 4, bit, lax.rem(w, 2)], ssem1, rsem1, (4 * t + 2 * core + b, 2 * half + 1 - bit)
        ).start()
        return c

    lax.fori_loop(0, 32, start1, 0)
    for d in (2, 3, 1):
        other = lax.rem(n + d, 4)
        remote(codes.at[pl.ds(4 * other, 4)], codes4.at[n], csend, crecv, (w, other)).start()
    own_codes = pltpu.make_async_copy(codes.at[pl.ds(4 * n, 4)], codes4.at[n], lsem.at[0])
    own_codes.start()

    load_x.wait()

    def group_rows(i, c):
        rows = xv[pl.ds(pl.multiple_of(64 * i, 64), 64), :].reshape(8, 8, 1024)
        for s in range(2):
            xrows[s, pl.ds(pl.multiple_of(32 * i, 32), 32), :] = rows[:, 4 * s : 4 * s + 4].reshape(32, 1024).astype(BF)
        return c

    lax.fori_loop(0, 16, group_rows, 0)

    pltpu.make_async_copy(send1, recv1.at[:, 1 - core], rsem1).wait()
    forward = remote(recv1.at[:, 1 - core], recv1.at[:, 1 - core], fsem1, gsem1, twin)
    forward.start()
    pltpu.make_async_copy(send1, recv1.at[:, core], gsem1).wait()
    for f in range(3):
        mixed = mm(xrows[core], recv1[:, :, :, f].reshape(1024, 128))
        send2[:, f] = mixed.reshape(128, 4, 128).astype(BF)

    def start2(i, c):
        to = lax.rem(chip + 1 + i, 128)
        remote(send2.at[to], recv2.at[chip], ssem2, rsem2, (to // 2, 2 * lax.rem(to, 2) + core)).start()
        return c

    lax.fori_loop(0, 127, start2, 0)
    own2 = pltpu.make_async_copy(send2.at[chip], recv2.at[chip], lsem.at[1])
    own2.start()

    for s in range(2):

        def flip(i, c):
            part = xrows[s, :, pl.ds(pl.multiple_of(128 * i, 128), 128)].astype(F32)
            xcols[s, pl.ds(2 * i, 2)] = part.T.reshape(2, 2, 32, 512).astype(BF)
            return c

        lax.fori_loop(0, 8, flip, 0)

    load_d.wait()
    pltpu.make_async_copy(codes4.at[0:3], codes4.at[0:3], crecv).wait()
    own_codes.wait()
    for m in range(4):
        atoms[:, 384 * m : 384 * m + 384] = mm(de[...], codes4[m].reshape(288, 384)).astype(BF)
    image = nt(atoms[...], dv[...])

    pltpu.make_async_copy(send2.at[0:127], recv2.at[0:127], rsem2).wait()
    own2.wait()
    got = recv2[...].reshape(16, 4, 2, 3, 4, 128)
    target = jnp.concatenate(
        [got[:, b, h].reshape(192, 128) for h in range(2) for b in range(4)], axis=1
    )
    misfit = (image - target.astype(F32)).astype(BF)
    for m in range(4):
        q = mm(misfit, dv[:, 384 * m : 384 * m + 384]).astype(BF)
        qsend[m] = q
        old = codes4[m].reshape(288, 384).astype(F32)
        fresh[m] = shrink(old, tn(de[...], q))
    for d in (2, 3, 1):
        other = lax.rem(n + d, 4)
        remote(qsend.at[other], qrecv.at[n], qssem, qrsem, (w, other)).start()
    own_q = pltpu.make_async_copy(qsend.at[n], qrecv.at[n], lsem.at[2])
    own_q.start()
    for m in range(4):
        atoms[:, 384 * m : 384 * m + 384] = mm(de[...], fresh[m]).astype(BF)
    for h in range(2):
        for b in range(4):
            block = nt(atoms[...], dv[512 * h + 128 * b : 512 * h + 128 * b + 128, :])
            send3[:, 2 * b + h] = block.reshape(16, 3, 4, 128).astype(BF)

    def start3(i, c):
        to = lax.rem(chip + 1 + i, 128)
        remote(
            send3.at[to // 8, lax.rem(to, 8)], recv3.at[core, chip], ssem3, rsem3, (to // 2, 2 * lax.rem(to, 2) + core)
        ).start()
        return c

    lax.fori_loop(0, 127, start3, 0)
    own3 = pltpu.make_async_copy(send3.at[chip // 8, lax.rem(chip, 8)], recv3.at[core, chip], lsem.at[3])
    own3.start()
    pltpu.make_async_copy(send2.at[0:127], recv3.at[core, 0:127], rsem3).wait()
    own3.wait()
    forward3 = remote(recv3.at[core], recv3.at[core], fsem3, gsem3, twin)
    forward3.start()
    pltpu.make_async_copy(send2, recv3.at[1 - core], gsem3).wait()

    for f in range(3):
        back = mm(xcols[0, :, 1 - core].reshape(512, 512), recv3[0, :, f].reshape(512, 128))
        back += mm(xcols[1, :, 1 - core].reshape(512, 512), recv3[1, :, f].reshape(512, 128))
        send4[:, :, f] = jnp.maximum(back, 0.0).reshape(16, 2, 16, 128).astype(BF)

    def start4(i, c):
        a = lax.rem(w // 4 + i // 2, 16)
        b = lax.rem(w + i, 2)
        to = 4 * a + 2 * (1 - core) + b
        remote(send4.at[a, b], recv4.at[w // 4, lax.rem(w, 2)], ssem4, rsem4, (to, 2 * half + bit)).start()
        return c

    lax.fori_loop(0, 32, start4, 0)

    pltpu.make_async_copy(qsend.at[0:3], qrecv.at[0:3], qrsem).wait()
    own_q.wait()
    for m in range(4):
        old = codes[4 * m : 4 * m + 4].reshape(288, 384).astype(F32)
        new_codes[4 * m : 4 * m + 4] = shrink(old, tn(de[...], qrecv[m])).reshape(4, 72, 384)

    pltpu.make_async_copy(send4, recv4, rsem4).wait()
    est[...] = recv4[...]

    pltpu.make_async_copy(send1, send1, ssem1).wait()
    pltpu.make_async_copy(send1, send1, fsem1).wait()
    pltpu.make_async_copy(send2.at[0:127], send2.at[0:127], ssem2).wait()
    pltpu.make_async_copy(send2.at[0:127], send2.at[0:127], ssem3).wait()
    pltpu.make_async_copy(send2, send2, fsem3).wait()
    pltpu.make_async_copy(send4, send4, ssem4).wait()
    pltpu.make_async_copy(codes4.at[0:3], codes4.at[0:3], csend).wait()
    pltpu.make_async_copy(qsend.at[0:3], qsend.at[0:3], qssem).wait()


def shards(volume, codes_in, x_transform, y_atoms, de_atoms):
    eye = jnp.eye(4, dtype=BF)
    de = (de_atoms[:, None, None, :] * eye[None, :, :, None]).reshape(192, 288)
    dma = pltpu.SemaphoreType.DMA
    vmem = pl.BlockSpec(memory_space=pltpu.VMEM)
    anyspace = pl.BlockSpec(memory_space=pl.ANY)
    codes_out, est = pl.pallas_call(
        kernel,
        out_shape=(
            jax.ShapeDtypeStruct((16, 72, 384), BF),
            jax.ShapeDtypeStruct((16, 2, 3, 16, 128), BF),
        ),
        in_specs=[vmem, vmem, anyspace, anyspace, vmem],
        out_specs=(vmem, vmem),
        scratch_shapes=[
            pltpu.VMEM((1024, 1024), F32),
            pltpu.VMEM((2, 512, 1024), BF),
            pltpu.VMEM((2, 16, 2, 32, 512), BF),
            pltpu.VMEM((1024, 1536), BF),
            pltpu.VMEM((4, 4, 72, 384), BF),
            pltpu.VMEM((16, 2, 3, 16, 128), BF),
            pltpu.VMEM((16, 2, 2, 3, 16, 128), BF),
            pltpu.VMEM((128, 3, 4, 128), BF),
            pltpu.VMEM((128, 3, 4, 128), BF),
            pltpu.VMEM((16, 8, 3, 4, 128), BF),
            pltpu.VMEM((2, 128, 3, 4, 128), BF),
            pltpu.VMEM((16, 2, 3, 16, 128), BF),
            pltpu.VMEM((16, 2, 3, 16, 128), BF),
            pltpu.VMEM((4, 192, 384), BF),
            pltpu.VMEM((4, 192, 384), BF),
            pltpu.VMEM((192, 1536), BF),
            pltpu.VMEM((4, 288, 384), BF),
            *[dma] * 18,
            dma((4,)),
        ],
        compiler_params=pltpu.CompilerParams(
            collective_id=0, has_side_effects=True, vmem_limit_bytes=60 * 1024 * 1024
        ),
    )(volume, codes_in, x_transform, y_atoms, de)
    estimate = est.transpose(3, 0, 2, 1, 4).reshape(16, 48, 256)
    return (codes_out, estimate)


def solution(mesh):
    return jax.shard_map(
        shards,
        mesh=mesh,
        in_specs=(P("wide", None, "narrow"), P("wide", None, "narrow"), P(), P(), P()),
        out_specs=(P("wide", None, "narrow"), P("wide", None, "narrow")),
        check_vma=False,
    )
```

time: 302 us -> 108 us (0.36)
  blocking collectives: 124 us -> 0 us
  waiting for transfers between devices: 116 us -> 0 us
  Pallas kernels: 0 us -> 101 us
  matrix products: 21.8 us -> 0 us
  local copies, waits for them, and re-layouts: 19.9 us -> 5.29 us
  between operations: 13.8 us -> 0.65 us
  starting transfers between devices: 5.94 us -> 0 us
    all_to_all x3 -> x0, blocking collectives: 124 us -> none  [the longest x2 102 us: along_x(): lax.all_to_all(flat, 'wide', split_axis=1, concat_axis=0, tiled=True)]
    pallas_call x0 -> x1, Pallas kernels: none -> 101 us  [shards(): pl.pallas_call(kernel, out_shape=(jax.ShapeDtypeStruct((16, 72, 384), BF)...]
    all_gather x3 -> x0, waiting for transfers between devices: 87.5 us -> none  [the longest x1 45.1 us: shards(): lax.all_gather(pulled, 'narrow', axis=2, tiled=True)]
    all_to_all x1 -> x0, waiting for transfers between devices: 28.1 us -> none  [along_x(): lax.all_to_all(mixed, 'wide', split_axis=0, concat_axis=1, tiled=True)]
    dot_general x8 -> x0, matrix products: 21.8 us -> none  [the longest x2 6.02 us: rebuild(): jnp.einsum('bfc,yc->bfy', lax.all_gather(atoms, 'narrow', axis=2, tiled=T...]
    all_to_all x5 -> x0, local copies, waits for them, and re-layouts: 11.8 us -> none  [the longest x4 8.96 us: along_x(): lax.all_to_all(flat, 'wide', split_axis=1, concat_axis=0, tiled=True)]
    all_to_all x1 -> x0, starting transfers between devices: 5.64 us -> none  [along_x(): lax.all_to_all(mixed, 'wide', split_axis=0, concat_axis=1, tiled=True)]
    convert_element_type x2 -> x0, local copies, waits for them, and re-layouts: 3.45 us -> none  [shards(): estimate = jnp.maximum(along_x(image, False), 0.0).astype(jnp.bfloat16)]
  transfers between devices with their start and end apart: 4 -> 0, of which waited for: 3 -> 0; matrix products, arithmetic and copies ran while one was open for 4% -> 0% of each run, Pallas kernels for 0% -> 0%
where the time goes in v1:
time: 108 us; the launch traced here: 107 us
  Pallas kernels  101 us (94%)
  local copies, waits for them, and re-layouts  5.29 us (5%)
    pallas_call x1, Pallas kernels, shards(): pl.pallas_call(kernel, out_shape=(jax.ShapeDtypeStruct((16, 72, 384), BF)...  101 us
    unnamed x1, local copies, waits for them, and re-layouts  2.17 us

profile of v1, /device:TPU:1, one launch (start us, length us, event | category | flops | bytes accessed | tf_op | source)
XLA Modules:
  0.0 107.4 jit_solution(13473491089381808882)
XLA Ops:
  0.6 0.9 broadcast_multiply_fusion
  1.5 0.8 mul.20.de
  2.3 100.6 %shard_map.68 = (bf16[16,72,384]{2,1,0:T(8,128)(2,1)}, bf16[16,2,3,16,128]{4,3,2,1,0:T(8,128)(2,1)}) custom-call(f32[16,48,256]{2,1,0:T(8,128)} %vol.1, bf16[16,72,384]{2,1,0:T(8,128)(2,1)} %codes.1, f32[1024,1024]{1,0:T(8,128)} %xin.1, bf16[1024,1536]{1,0:T(8,128)(2,1)} %din.1, bf16[192,288]{1,0:T(8,128)(2,1)} %mul.20.de), custom_call_target="tpu_custom_call" | custom-call | tf_op jit(solution)/shard_map/pallas_call | solution.py:219
  102.9 1.3 %copy.7 = bf16[16,16,3,2,128]{4,3,2,1,0:T(2,128)(2,1)S(1)} copy(bf16[16,16,3,2,128]{4,0,2,3,1:T(8,128)(2,1)} %bitcast.1) | data formatting | bytes 786432 | tf_op jit(solution)/shard_map/transpose | solution.py:252
  104.2 1.0 reshape.20
  105.2 2.2 %copy.9 = bf16[16,72,384]{2,1,0:T(8,128)(2,1)} copy(bf16[16,72,384]{2,1,0:T(8,128)(2,1)} %get-tuple-element.8) | data formatting | bytes 1769472
  (1 shorter events, 0.0 us)

commit v2 on v1

--- a/solution.py
+++ b/solution.py
@@ -36,10 +36,10 @@
 
 
 def kernel(
-    vol, codes, xin, din, de,
-    new_codes, est,
-    xv, xrows, xcols, dv, codes4, send1, recv1, send2, recv2, send3, recv3, send4, recv4, qsend, qrecv, atoms, fresh,
-    xsem, dsem, ssem1, rsem1, fsem1, gsem1, ssem2, rsem2, ssem3, rsem3, fsem3, gsem3, ssem4, rsem4,
+    vol_in, codes, xin, din, de_in,
+    new_low, new_high, est,
+    vol, mine, new, de_small, de, xv, xrows, xcols, dv, codes4, send1, recv1, send2, recv2, send3, recv3, send4, recv4, qsend, qrecv, atoms, fresh,
+    load, ssem1, rsem1, fsem1, gsem1, ssem2, rsem2, ssem3, rsem3, fsem3, gsem3, ssem4, rsem4,
     csend, crecv, qssem, qrsem, lsem,
 ):
     w = lax.axis_index("wide")
@@ -50,17 +50,15 @@
     twin = (w, 2 * half + 1 - core)
     bit = lax.rem(w // 2, 2)
 
-    load_x = pltpu.make_async_copy(xin, xv, xsem)
-    load_d = pltpu.make_async_copy(din, dv, dsem)
-    load_x.start()
-    load_d.start()
+    loads = [
+        pltpu.make_async_copy(src, dst, load.at[i])
+        for i, (src, dst) in enumerate(((vol_in, vol), (xin, xv), (de_in, de_small), (din, dv), (codes, mine)))
+    ]
+    load_vol, load_x, load_de, load_d, load_codes = loads
+    for copy in loads:
+        copy.start()
 
     barrier = pltpu.get_barrier_semaphore()
-
-    def greet_to(i, c):
-        to = 4 * (i // 2) + 2 * core + lax.rem(i, 2)
-        pl.semaphore_signal(barrier, inc=1, device_id=(to, 2 * half + 1 - bit), device_id_type=MESH)
-        return c
 
     def greet_from(i, c):
         frm = 4 * (i // 2) + 2 * (1 - core) + lax.rem(i, 2)
@@ -69,15 +67,15 @@
 
     for d in (1, 2, 3):
         pl.semaphore_signal(barrier, inc=1, device_id=(w, lax.rem(n + d, 4)), device_id_type=MESH)
-    lax.fori_loop(0, 32, greet_to, 0)
     lax.fori_loop(0, 32, greet_from, 0)
 
+    load_vol.wait()
     for f in range(48):
         rows = vol[:, f, :].astype(BF)
         for b in range(2):
             send1[f // 3, b, f % 3] = rows[:, 128 * b : 128 * b + 128]
 
-    pl.semaphore_wait(barrier, 67)
+    pl.semaphore_wait(barrier, 35)
 
     def start1(i, c):
         t = lax.rem(w // 4 + i // 2, 16)
@@ -90,7 +88,9 @@
     lax.fori_loop(0, 32, start1, 0)
     for d in (2, 3, 1):
         other = lax.rem(n + d, 4)
-        remote(codes.at[pl.ds(4 * other, 4)], codes4.at[n], csend, crecv, (w, other)).start()
+        remote(
+            codes.at[pl.ds(4 * other, 2)], codes4.at[n, 0:2], csend.at[0], crecv.at[0], (w, other)
+        ).start()
     own_codes = pltpu.make_async_copy(codes.at[pl.ds(4 * n, 4)], codes4.at[n], lsem.at[0])
     own_codes.start()
 
@@ -104,7 +104,20 @@
 
     lax.fori_loop(0, 16, group_rows, 0)
 
+    load_de.wait()
+    spread = (lax.broadcasted_iota(jnp.int32, (192, 48), 0) // 4 == lax.broadcasted_iota(jnp.int32, (192, 48), 1))
+    tile = (lax.rem(lax.broadcasted_iota(jnp.int32, (72, 288), 1), 72) == lax.broadcasted_iota(jnp.int32, (72, 288), 0))
+    tall = mm(spread.astype(F32).astype(BF), de_small[...]).astype(BF)
+    wide = mm(tall, tile.astype(F32).astype(BF))
+    same = lax.rem(lax.broadcasted_iota(jnp.int32, (192, 288), 0), 4) == lax.broadcasted_iota(jnp.int32, (192, 288), 1) // 72
+    de[...] = jnp.where(same, wide, 0.0).astype(BF)
+
     pltpu.make_async_copy(send1, recv1.at[:, 1 - core], rsem1).wait()
+    for d in (2, 3, 1):
+        other = lax.rem(n + d, 4)
+        remote(
+            codes.at[pl.ds(4 * other + 2, 2)], codes4.at[n, 2:4], csend.at[1], crecv.at[1], (w, other)
+        ).start()
     forward = remote(recv1.at[:, 1 - core], recv1.at[:, 1 - core], fsem1, gsem1, twin)
     forward.start()
     pltpu.make_async_copy(send1, recv1.at[:, core], gsem1).wait()
@@ -131,7 +144,8 @@
         lax.fori_loop(0, 8, flip, 0)
 
     load_d.wait()
-    pltpu.make_async_copy(codes4.at[0:3], codes4.at[0:3], crecv).wait()
+    pltpu.make_async_copy(codes4.at[0:3, 0:2], codes4.at[0:3, 0:2], crecv.at[0]).wait()
+    pltpu.make_async_copy(codes4.at[0:3, 2:4], codes4.at[0:3, 2:4], crecv.at[1]).wait()
     own_codes.wait()
     for m in range(4):
         atoms[:, 384 * m : 384 * m + 384] = mm(de[...], codes4[m].reshape(288, 384)).astype(BF)
@@ -144,14 +158,15 @@
         [got[:, b, h].reshape(192, 128) for h in range(2) for b in range(4)], axis=1
     )
     misfit = (image - target.astype(F32)).astype(BF)
+    for d in (2, 3, 1, 0):
+        m = n ^ d
+        q = mm(misfit, dv[:, pl.ds(pl.multiple_of(384 * m, 384), 384)]).astype(BF)
+        qsend[m] = q
+        if d:
+            remote(qsend.at[m, 0:64], qrecv.at[n, 0:64], qssem.at[0], qrsem.at[0], (w, m)).start()
     for m in range(4):
-        q = mm(misfit, dv[:, 384 * m : 384 * m + 384]).astype(BF)
-        qsend[m] = q
         old = codes4[m].reshape(288, 384).astype(F32)
-        fresh[m] = shrink(old, tn(de[...], q))
-    for d in (2, 3, 1):
-        other = lax.rem(n + d, 4)
-        remote(qsend.at[other], qrecv.at[n], qssem, qrsem, (w, other)).start()
+        fresh[m] = shrink(old, tn(de[...], qsend[m]))
     own_q = pltpu.make_async_copy(qsend.at[n], qrecv.at[n], lsem.at[2])
     own_q.start()
     for m in range(4):
@@ -172,6 +187,9 @@
     own3 = pltpu.make_async_copy(send3.at[chip // 8, lax.rem(chip, 8)], recv3.at[core, chip], lsem.at[3])
     own3.start()
     pltpu.make_async_copy(send2.at[0:127], recv3.at[core, 0:127], rsem3).wait()
+    for d in (2, 3, 1):
+        other = lax.rem(n + d, 4)
+        remote(qsend.at[other, 64:192], qrecv.at[n, 64:192], qssem.at[1], qrsem.at[1], (w, other)).start()
     own3.wait()
     forward3 = remote(recv3.at[core], recv3.at[core], fsem3, gsem3, twin)
     forward3.start()
@@ -191,14 +209,21 @@
 
     lax.fori_loop(0, 32, start4, 0)
 
-    pltpu.make_async_copy(qsend.at[0:3], qrecv.at[0:3], qrsem).wait()
+    pltpu.make_async_copy(qsend.at[0:3, 0:64], qrecv.at[0:3, 0:64], qrsem.at[0]).wait()
+    pltpu.make_async_copy(qsend.at[0:3, 64:192], qrecv.at[0:3, 64:192], qrsem.at[1]).wait()
+    load_codes.wait()
     own_q.wait()
     for m in range(4):
-        old = codes[4 * m : 4 * m + 4].reshape(288, 384).astype(F32)
-        new_codes[4 * m : 4 * m + 4] = shrink(old, tn(de[...], qrecv[m])).reshape(4, 72, 384)
-
+        old = mine[4 * m : 4 * m + 4].reshape(288, 384).astype(F32)
+        new[4 * m : 4 * m + 4] = shrink(old, tn(de[...], qrecv[m])).reshape(4, 72, 384)
+
+    put_low = pltpu.make_async_copy(new.at[0:8], new_low, lsem.at[4])
+    put_high = pltpu.make_async_copy(new.at[8:16], new_high, lsem.at[6])
+    put_low.start()
+    put_high.start()
     pltpu.make_async_copy(send4, recv4, rsem4).wait()
-    est[...] = recv4[...]
+    put_est = pltpu.make_async_copy(recv4, est, lsem.at[5])
+    put_est.start()
 
     pltpu.make_async_copy(send1, send1, ssem1).wait()
     pltpu.make_async_copy(send1, send1, fsem1).wait()
@@ -206,25 +231,49 @@
     pltpu.make_async_copy(send2.at[0:127], send2.at[0:127], ssem3).wait()
     pltpu.make_async_copy(send2, send2, fsem3).wait()
     pltpu.make_async_copy(send4, send4, ssem4).wait()
-    pltpu.make_async_copy(codes4.at[0:3], codes4.at[0:3], csend).wait()
-    pltpu.make_async_copy(qsend.at[0:3], qsend.at[0:3], qssem).wait()
+    pltpu.make_async_copy(codes4.at[0:3, 0:2], codes4.at[0:3, 0:2], csend.at[0]).wait()
+    pltpu.make_async_copy(codes4.at[0:3, 2:4], codes4.at[0:3, 2:4], csend.at[1]).wait()
+    pltpu.make_async_copy(qsend.at[0:3, 0:64], qsend.at[0:3, 0:64], qssem.at[0]).wait()
+    pltpu.make_async_copy(qsend.at[0:3, 64:192], qsend.at[0:3, 64:192], qssem.at[1]).wait()
+    put_low.wait()
+    put_high.wait()
+    put_est.wait()
+
+
+def finish(low, high, est, codes_out, estimate, flat, out, sem):
+    put_low = pltpu.make_async_copy(low, codes_out.at[0:8], sem.at[0])
+    put_high = pltpu.make_async_copy(high, codes_out.at[8:16], sem.at[2])
+    put_low.start()
+    put_high.start()
+    for b in range(2):
+        for f in range(48):
+            flat[:, f] = est[f // 3, b, f % 3].astype(F32)
+        out[:, :, 128 * b : 128 * b + 128] = flat[...].astype(BF)
+    put_est = pltpu.make_async_copy(out, estimate, sem.at[1])
+    put_est.start()
+    put_low.wait()
+    put_high.wait()
+    put_est.wait()
 
 
 def shards(volume, codes_in, x_transform, y_atoms, de_atoms):
-    eye = jnp.eye(4, dtype=BF)
-    de = (de_atoms[:, None, None, :] * eye[None, :, :, None]).reshape(192, 288)
     dma = pltpu.SemaphoreType.DMA
-    vmem = pl.BlockSpec(memory_space=pltpu.VMEM)
     anyspace = pl.BlockSpec(memory_space=pl.ANY)
-    codes_out, est = pl.pallas_call(
+    low, high, est = pl.pallas_call(
         kernel,
         out_shape=(
-            jax.ShapeDtypeStruct((16, 72, 384), BF),
+            jax.ShapeDtypeStruct((8, 72, 384), BF),
+            jax.ShapeDtypeStruct((8, 72, 384), BF),
             jax.ShapeDtypeStruct((16, 2, 3, 16, 128), BF),
         ),
-        in_specs=[vmem, vmem, anyspace, anyspace, vmem],
-        out_specs=(vmem, vmem),
+        in_specs=[anyspace] * 5,
+        out_specs=(anyspace, anyspace, anyspace),
         scratch_shapes=[
+            pltpu.VMEM((16, 48, 256), F32),
+            pltpu.VMEM((16, 72, 384), BF),
+            pltpu.VMEM((16, 72, 384), BF),
+            pltpu.VMEM((48, 72), BF),
+            pltpu.VMEM((192, 288), BF),
             pltpu.VMEM((1024, 1024), F32),
             pltpu.VMEM((2, 512, 1024), BF),
             pltpu.VMEM((2, 16, 2, 32, 512), BF),
@@ -242,15 +291,30 @@
             pltpu.VMEM((4, 192, 384), BF),
             pltpu.VMEM((192, 1536), BF),
             pltpu.VMEM((4, 288, 384), BF),
-            *[dma] * 18,
-            dma((4,)),
+            dma((5,)),
+            *[dma] * 12,
+            *[dma((2,))] * 4,
+            dma((7,)),
         ],
         compiler_params=pltpu.CompilerParams(
-            collective_id=0, has_side_effects=True, vmem_limit_bytes=60 * 1024 * 1024
+            collective_id=0, has_side_effects=True, vmem_limit_bytes=54850000
         ),
-    )(volume, codes_in, x_transform, y_atoms, de)
-    estimate = est.transpose(3, 0, 2, 1, 4).reshape(16, 48, 256)
-    return (codes_out, estimate)
+    )(volume, codes_in, x_transform, y_atoms, de_atoms)
+    return pl.pallas_call(
+        finish,
+        out_shape=(
+            jax.ShapeDtypeStruct((16, 72, 384), BF),
+            jax.ShapeDtypeStruct((16, 48, 256), BF),
+        ),
+        in_specs=[pl.BlockSpec(memory_space=pltpu.VMEM)] * 3,
+        out_specs=(anyspace, anyspace),
+        scratch_shapes=[
+            pltpu.VMEM((16, 48, 128), F32),
+            pltpu.VMEM((16, 48, 256), BF),
+            dma((3,)),
+        ],
+        compiler_params=pltpu.CompilerParams(vmem_limit_bytes=8 * 1024 * 1024),
+    )(low, high, est)
 
 
 def solution(mesh):

time: 108 us -> 96 us (0.89)
  Pallas kernels: 101 us -> 94.5 us
  local copies, waits for them, and re-layouts: 5.29 us -> 0.7 us
    pallas_call x1 -> x2, Pallas kernels: 101 us -> 94.5 us  [the longest x1 93.2 us: shards(): pl.pallas_call(kernel, out_shape=(jax.ShapeDtypeStruct((8, 72, 384), BF),...]
    unnamed x1 -> x2, local copies, waits for them, and re-layouts: 2.17 us -> 0.7 us
    transpose x1 -> x0, local copies, waits for them, and re-layouts: 1.3 us -> none  [shards(): estimate = est.transpose(3, 0, 2, 1, 4).reshape(16, 48, 256)]
where the time goes in v2:
time: 96 us; the launch traced here: 95.8 us
  Pallas kernels  94.5 us (98%)
    pallas_call x1, Pallas kernels, shards(): pl.pallas_call(kernel, out_shape=(jax.ShapeDtypeStruct((8, 72, 384), BF),...  93.2 us

profile of v2, /device:TPU:1, one launch (start us, length us, event | category | flops | bytes accessed | tf_op | source)
XLA Modules:
  0.0 95.8 jit_solution(17287432520433993134)
XLA Ops:
  0.6 0.0 copy-start
  0.6 0.7 copy-done
  1.3 93.2 %shard_map.68 = (bf16[8,72,384]{2,1,0:T(8,128)(2,1)S(1)}, bf16[8,72,384]{2,1,0:T(8,128)(2,1)S(1)}, bf16[16,2,3,16,128]{4,3,2,1,0:T(8,128)(2,1)S(1)}) custom-call(f32[16,48,256]{2,1,0:T(8,128)} %vol_in.1, bf16[16,72,384]{2,1,0:T(8,128)(2,1)} %codes.1, f32[1024,1024]{1,0:T(8,128)} %xin.1, bf16[1024,1536]{1,0:T(8,128)(2,1)} %din.1, bf16[48,72]{1,0:T(8,128)(2,1)S(1)} %copy-done), custom_call_target="tpu_custom_call" | custom-call | tf_op jit(solution)/shard_map/pallas_call | solution.py:262
  94.6 1.3 %shard_map.69 = (bf16[16,72,384]{2,1,0:T(8,128)(2,1)}, bf16[16,48,256]{2,1,0:T(8,128)(2,1)}) custom-call(bf16[8,72,384]{2,1,0:T(8,128)(2,1)S(1)} %get-tuple-element.5.low, bf16[8,72,384]{2,1,0:T(8,128)(2,1)S(1)} %get-tuple-element.6.high, bf16[16,2,3,16,128]{4,3,2,1,0:T(8,128)(2,1)S(1)} %get-tuple-element.7.est), custom_call_target="tpu_custom_call" | custom-call | tf_op jit(solution)/shard_map/pallas_call | solution.py:303
Async XLA Ops:
  0.6 0.7 copy-start

commit v3 on v2

--- a/solution.py
+++ b/solution.py
@@ -40,7 +40,7 @@
     new_low, new_high, est,
     vol, mine, new, de_small, de, xv, xrows, xcols, dv, codes4, send1, recv1, send2, recv2, send3, recv3, send4, recv4, qsend, qrecv, atoms, fresh,
     load, ssem1, rsem1, fsem1, gsem1, ssem2, rsem2, ssem3, rsem3, fsem3, gsem3, ssem4, rsem4,
-    csend, crecv, qssem, qrsem, lsem,
+    csend, crecv, qssem, qrsem, lsem, msem, relays, mid, midq,
 ):
     w = lax.axis_index("wide")
     n = lax.axis_index("narrow")
@@ -49,6 +49,16 @@
     chip = 2 * w + half
     twin = (w, 2 * half + 1 - core)
     bit = lax.rem(w // 2, 2)
+    low = lax.rem(w, 4)
+    across = w - low + lax.rem(low + 2, 4)
+    up_half = lax.rem(half + low // 2, 2)
+    down_half = 1 - up_half
+    up = (across, 2 * up_half + core)
+    down = (across, 2 * down_half + core)
+    down_other = (across, 2 * down_half + 1 - core)
+    near = n + 1 - 2 * core
+    facing = lax.rem(n + 2, 4)
+    cross = 2 * (1 - half) + 1 - core
 
     loads = [
         pltpu.make_async_copy(src, dst, load.at[i])
@@ -67,6 +77,8 @@
 
     for d in (1, 2, 3):
         pl.semaphore_signal(barrier, inc=1, device_id=(w, lax.rem(n + d, 4)), device_id_type=MESH)
+    for to in (up, down, (across, 2 * up_half + 1 - core)):
+        pl.semaphore_signal(barrier, inc=1, device_id=to, device_id_type=MESH)
     lax.fori_loop(0, 32, greet_from, 0)
 
     load_vol.wait()
@@ -75,7 +87,7 @@
         for b in range(2):
             send1[f // 3, b, f % 3] = rows[:, 128 * b : 128 * b + 128]
 
-    pl.semaphore_wait(barrier, 35)
+    pl.semaphore_wait(barrier, 38)
 
     def start1(i, c):
         t = lax.rem(w // 4 + i // 2, 16)
@@ -86,11 +98,13 @@
         return c
 
     lax.fori_loop(0, 32, start1, 0)
-    for d in (2, 3, 1):
-        other = lax.rem(n + d, 4)
-        remote(
-            codes.at[pl.ds(4 * other, 2)], codes4.at[n, 0:2], csend.at[0], crecv.at[0], (w, other)
-        ).start()
+    remote(codes.at[4 * facing + 0], mid.at[0, 0], csend.at[0], msem.at[0, 0], up).start()
+    remote(codes.at[4 * cross + 0], mid.at[1, 0], csend.at[0], msem.at[1, 0], down).start()
+    remote(codes.at[4 * facing + 1], mid.at[0, 1], csend.at[0], msem.at[0, 1], up).start()
+    remote(codes.at[4 * cross + 1], mid.at[1, 1], csend.at[0], msem.at[1, 1], down).start()
+    remote(codes.at[4 * facing + 2], mid.at[0, 2], csend.at[0], msem.at[0, 2], up).start()
+    remote(codes.at[4 * cross + 2], mid.at[1, 2], csend.at[0], msem.at[1, 2], down).start()
+    remote(codes.at[pl.ds(4 * near + 0, 3)], codes4.at[n, 0:3], csend.at[0], crecv.at[0], (w, near)).start()
     own_codes = pltpu.make_async_copy(codes.at[pl.ds(4 * n, 4)], codes4.at[n], lsem.at[0])
     own_codes.start()
 
@@ -112,14 +126,24 @@
     same = lax.rem(lax.broadcasted_iota(jnp.int32, (192, 288), 0), 4) == lax.broadcasted_iota(jnp.int32, (192, 288), 1) // 72
     de[...] = jnp.where(same, wide, 0.0).astype(BF)
 
+    pltpu.make_async_copy(mid.at[0, 0], mid.at[0, 0], msem.at[0, 0]).wait()
+    remote(mid.at[0, 0], codes4.at[2 * down_half + core, 0], relays.at[0], crecv.at[0], up).start()
+    pltpu.make_async_copy(mid.at[1, 0], mid.at[1, 0], msem.at[1, 0]).wait()
+    remote(mid.at[1, 0], codes4.at[2 * up_half + core, 0], relays.at[0], crecv.at[0], down_other).start()
+    pltpu.make_async_copy(mid.at[0, 1], mid.at[0, 1], msem.at[0, 1]).wait()
+    remote(mid.at[0, 1], codes4.at[2 * down_half + core, 1], relays.at[0], crecv.at[0], up).start()
+    pltpu.make_async_copy(mid.at[1, 1], mid.at[1, 1], msem.at[1, 1]).wait()
+    remote(mid.at[1, 1], codes4.at[2 * up_half + core, 1], relays.at[0], crecv.at[0], down_other).start()
+    pltpu.make_async_copy(mid.at[0, 2], mid.at[0, 2], msem.at[0, 2]).wait()
+    remote(mid.at[0, 2], codes4.at[2 * down_half + core, 2], relays.at[0], crecv.at[0], up).start()
+    pltpu.make_async_copy(mid.at[1, 2], mid.at[1, 2], msem.at[1, 2]).wait()
+    remote(mid.at[1, 2], codes4.at[2 * up_half + core, 2], relays.at[0], crecv.at[0], down_other).start()
     pltpu.make_async_copy(send1, recv1.at[:, 1 - core], rsem1).wait()
-    for d in (2, 3, 1):
-        other = lax.rem(n + d, 4)
-        remote(
-            codes.at[pl.ds(4 * other + 2, 2)], codes4.at[n, 2:4], csend.at[1], crecv.at[1], (w, other)
-        ).start()
     forward = remote(recv1.at[:, 1 - core], recv1.at[:, 1 - core], fsem1, gsem1, twin)
     forward.start()
+    remote(codes.at[4 * facing + 3], mid.at[0, 3], csend.at[1], msem.at[0, 3], up).start()
+    remote(codes.at[4 * cross + 3], mid.at[1, 3], csend.at[1], msem.at[1, 3], down).start()
+    remote(codes.at[pl.ds(4 * near + 3, 1)], codes4.at[n, 3:4], csend.at[1], crecv.at[1], (w, near)).start()
     pltpu.make_async_copy(send1, recv1.at[:, core], gsem1).wait()
     for f in range(3):
         mixed = mm(xrows[core], recv1[:, :, :, f].reshape(1024, 128))
@@ -133,6 +157,10 @@
     lax.fori_loop(0, 127, start2, 0)
     own2 = pltpu.make_async_copy(send2.at[chip], recv2.at[chip], lsem.at[1])
     own2.start()
+    pltpu.make_async_copy(mid.at[0, 3], mid.at[0, 3], msem.at[0, 3]).wait()
+    remote(mid.at[0, 3], codes4.at[2 * down_half + core, 3], relays.at[0], crecv.at[1], up).start()
+    pltpu.make_async_copy(mid.at[1, 3], mid.at[1, 3], msem.at[1, 3]).wait()
+    remote(mid.at[1, 3], codes4.at[2 * up_half + core, 3], relays.at[0], crecv.at[1], down_other).start()
 
     for s in range(2):
 
@@ -144,8 +172,8 @@
         lax.fori_loop(0, 8, flip, 0)
 
     load_d.wait()
-    pltpu.make_async_copy(codes4.at[0:3, 0:2], codes4.at[0:3, 0:2], crecv.at[0]).wait()
-    pltpu.make_async_copy(codes4.at[0:3, 2:4], codes4.at[0:3, 2:4], crecv.at[1]).wait()
+    pltpu.make_async_copy(codes4.at[0:3, 0:3], codes4.at[0:3, 0:3], crecv.at[0]).wait()
+    pltpu.make_async_copy(codes4.at[0:3, 3:4], codes4.at[0:3, 3:4], crecv.at[1]).wait()
     own_codes.wait()
     for m in range(4):
         atoms[:, 384 * m : 384 * m + 384] = mm(de[...], codes4[m].reshape(288, 384)).astype(BF)
@@ -162,8 +190,12 @@
         m = n ^ d
         q = mm(misfit, dv[:, pl.ds(pl.multiple_of(384 * m, 384), 384)]).astype(BF)
         qsend[m] = q
-        if d:
-            remote(qsend.at[m, 0:64], qrecv.at[n, 0:64], qssem.at[0], qrsem.at[0], (w, m)).start()
+        if d == 2:
+            remote(qsend.at[m, 0:128], midq.at[0, 0:128], qssem.at[0], msem.at[0, 4], up).start()
+        elif d == 3:
+            remote(qsend.at[m, 0:128], midq.at[1, 0:128], qssem.at[0], msem.at[1, 4], down).start()
+        elif d == 1:
+            remote(qsend.at[m, 0:128], qrecv.at[n, 0:128], qssem.at[0], qrsem.at[0], (w, m)).start()
     for m in range(4):
         old = codes4[m].reshape(288, 384).astype(F32)
         fresh[m] = shrink(old, tn(de[...], qsend[m]))
@@ -186,13 +218,19 @@
     lax.fori_loop(0, 127, start3, 0)
     own3 = pltpu.make_async_copy(send3.at[chip // 8, lax.rem(chip, 8)], recv3.at[core, chip], lsem.at[3])
     own3.start()
+    pltpu.make_async_copy(midq.at[0, 0:128], midq.at[0, 0:128], msem.at[0, 4]).wait()
+    remote(midq.at[0, 0:128], qrecv.at[2 * down_half + core, 0:128], relays.at[1], qrsem.at[0], up).start()
+    pltpu.make_async_copy(midq.at[1, 0:128], midq.at[1, 0:128], msem.at[1, 4]).wait()
+    remote(midq.at[1, 0:128], qrecv.at[2 * up_half + core, 0:128], relays.at[1], qrsem.at[0], down_other).start()
     pltpu.make_async_copy(send2.at[0:127], recv3.at[core, 0:127], rsem3).wait()
-    for d in (2, 3, 1):
-        other = lax.rem(n + d, 4)
-        remote(qsend.at[other, 64:192], qrecv.at[n, 64:192], qssem.at[1], qrsem.at[1], (w, other)).start()
     own3.wait()
     forward3 = remote(recv3.at[core], recv3.at[core], fsem3, gsem3, twin)
     forward3.start()
+    remote(qsend.at[facing, 128:160], midq.at[0, 128:160], qssem.at[1], msem.at[0, 5], up).start()
+    remote(qsend.at[cross, 128:160], midq.at[1, 128:160], qssem.at[1], msem.at[1, 5], down).start()
+    remote(qsend.at[facing, 160:192], midq.at[0, 160:192], qssem.at[1], msem.at[0, 6], up).start()
+    remote(qsend.at[cross, 160:192], midq.at[1, 160:192], qssem.at[1], msem.at[1, 6], down).start()
+    remote(qsend.at[near, 128:192], qrecv.at[n, 128:192], qssem.at[1], qrsem.at[1], (w, near)).start()
     pltpu.make_async_copy(send2, recv3.at[1 - core], gsem3).wait()
 
     for f in range(3):
@@ -208,9 +246,17 @@
         return c
 
     lax.fori_loop(0, 32, start4, 0)
-
-    pltpu.make_async_copy(qsend.at[0:3, 0:64], qrecv.at[0:3, 0:64], qrsem.at[0]).wait()
-    pltpu.make_async_copy(qsend.at[0:3, 64:192], qrecv.at[0:3, 64:192], qrsem.at[1]).wait()
+    pltpu.make_async_copy(midq.at[0, 128:160], midq.at[0, 128:160], msem.at[0, 5]).wait()
+    remote(midq.at[0, 128:160], qrecv.at[2 * down_half + core, 128:160], relays.at[1], qrsem.at[1], up).start()
+    pltpu.make_async_copy(midq.at[1, 128:160], midq.at[1, 128:160], msem.at[1, 5]).wait()
+    remote(midq.at[1, 128:160], qrecv.at[2 * up_half + core, 128:160], relays.at[1], qrsem.at[1], down_other).start()
+    pltpu.make_async_copy(midq.at[0, 160:192], midq.at[0, 160:192], msem.at[0, 6]).wait()
+    remote(midq.at[0, 160:192], qrecv.at[2 * down_half + core, 160:192], relays.at[1], qrsem.at[1], up).start()
+    pltpu.make_async_copy(midq.at[1, 160:192], midq.at[1, 160:192], msem.at[1, 6]).wait()
+    remote(midq.at[1, 160:192], qrecv.at[2 * up_half + core, 160:192], relays.at[1], qrsem.at[1], down_other).start()
+
+    pltpu.make_async_copy(qsend.at[0:3, 0:128], qrecv.at[0:3, 0:128], qrsem.at[0]).wait()
+    pltpu.make_async_copy(qsend.at[0:3, 128:192], qrecv.at[0:3, 128:192], qrsem.at[1]).wait()
     load_codes.wait()
     own_q.wait()
     for m in range(4):
@@ -231,10 +277,12 @@
     pltpu.make_async_copy(send2.at[0:127], send2.at[0:127], ssem3).wait()
     pltpu.make_async_copy(send2, send2, fsem3).wait()
     pltpu.make_async_copy(send4, send4, ssem4).wait()
-    pltpu.make_async_copy(codes4.at[0:3, 0:2], codes4.at[0:3, 0:2], csend.at[0]).wait()
-    pltpu.make_async_copy(codes4.at[0:3, 2:4], codes4.at[0:3, 2:4], csend.at[1]).wait()
-    pltpu.make_async_copy(qsend.at[0:3, 0:64], qsend.at[0:3, 0:64], qssem.at[0]).wait()
-    pltpu.make_async_copy(qsend.at[0:3, 64:192], qsend.at[0:3, 64:192], qssem.at[1]).wait()
+    pltpu.make_async_copy(codes4.at[0:3, 0:3], codes4.at[0:3, 0:3], csend.at[0]).wait()
+    pltpu.make_async_copy(codes4.at[0:3, 3:4], codes4.at[0:3, 3:4], csend.at[1]).wait()
+    pltpu.make_async_copy(qsend.at[0:3, 0:128], qsend.at[0:3, 0:128], qssem.at[0]).wait()
+    pltpu.make_async_copy(qsend.at[0:3, 128:192], qsend.at[0:3, 128:192], qssem.at[1]).wait()
+    pltpu.make_async_copy(mid, mid, relays.at[0]).wait()
+    pltpu.make_async_copy(midq, midq, relays.at[1]).wait()
     put_low.wait()
     put_high.wait()
     put_est.wait()
@@ -295,6 +343,10 @@
             *[dma] * 12,
             *[dma((2,))] * 4,
             dma((7,)),
+            dma((2, 7)),
+            dma((2,)),
+            pltpu.VMEM((2, 4, 72, 384), BF),
+            pltpu.VMEM((2, 192, 384), BF),
         ],
         compiler_params=pltpu.CompilerParams(
             collective_id=0, has_side_effects=True, vmem_limit_bytes=54850000

time: 96 us -> 89.1 us (0.928)
  Pallas kernels: 94.5 us -> 87.6 us
    pallas_call x1, Pallas kernels: 93.2 us -> 86.3 us  [shards(): pl.pallas_call(kernel, out_shape=(jax.ShapeDtypeStruct((8, 72, 384), BF),...]
where the time goes in v3:
time: 89.1 us; the launch traced here: 88.9 us
  Pallas kernels  87.6 us (98%)
    pallas_call x1, Pallas kernels, shards(): pl.pallas_call(kernel, out_shape=(jax.ShapeDtypeStruct((8, 72, 384), BF),...  86.3 us

profile of v3, /device:TPU:1, one launch (start us, length us, event | category | flops | bytes accessed | tf_op | source)
XLA Modules:
  0.0 88.9 jit_solution(5573554950697479214)
XLA Ops:
  0.6 0.0 copy-start
  0.6 0.7 copy-done
  1.3 86.3 %shard_map.68 = (bf16[8,72,384]{2,1,0:T(8,128)(2,1)S(1)}, bf16[8,72,384]{2,1,0:T(8,128)(2,1)S(1)}, bf16[16,2,3,16,128]{4,3,2,1,0:T(8,128)(2,1)S(1)}) custom-call(f32[16,48,256]{2,1,0:T(8,128)} %vol_in.1, bf16[16,72,384]{2,1,0:T(8,128)(2,1)} %codes.1, f32[1024,1024]{1,0:T(8,128)} %xin.1, bf16[1024,1536]{1,0:T(8,128)(2,1)} %din.1, bf16[48,72]{1,0:T(8,128)(2,1)S(1)} %copy-done), custom_call_target="tpu_custom_call" | custom-call | tf_op jit(solution)/shard_map/pallas_call | solution.py:310
  87.7 1.3 %shard_map.69 = (bf16[16,72,384]{2,1,0:T(8,128)(2,1)}, bf16[16,48,256]{2,1,0:T(8,128)(2,1)}) custom-call(bf16[8,72,384]{2,1,0:T(8,128)(2,1)S(1)} %get-tuple-element.5.low, bf16[8,72,384]{2,1,0:T(8,128)(2,1)S(1)} %get-tuple-element.6.high, bf16[16,2,3,16,128]{4,3,2,1,0:T(8,128)(2,1)S(1)} %get-tuple-element.7.est), custom_call_target="tpu_custom_call" | custom-call | tf_op jit(solution)/shard_map/pallas_call | solution.py:355
Async XLA Ops:
  0.6 0.7 copy-start

commit v4 on v3

--- a/solution.py
+++ b/solution.py
@@ -65,8 +65,7 @@
         for i, (src, dst) in enumerate(((vol_in, vol), (xin, xv), (de_in, de_small), (din, dv), (codes, mine)))
     ]
     load_vol, load_x, load_de, load_d, load_codes = loads
-    for copy in loads:
-        copy.start()
+    load_vol.start()
 
     barrier = pltpu.get_barrier_semaphore()
 
@@ -81,6 +80,8 @@
         pl.semaphore_signal(barrier, inc=1, device_id=to, device_id_type=MESH)
     lax.fori_loop(0, 32, greet_from, 0)
 
+    for copy in loads[1:]:
+        copy.start()
     load_vol.wait()
     for f in range(48):
         rows = vol[:, f, :].astype(BF)
@@ -105,6 +106,9 @@
     remote(codes.at[4 * facing + 2], mid.at[0, 2], csend.at[0], msem.at[0, 2], up).start()
     remote(codes.at[4 * cross + 2], mid.at[1, 2], csend.at[0], msem.at[1, 2], down).start()
     remote(codes.at[pl.ds(4 * near + 0, 3)], codes4.at[n, 0:3], csend.at[0], crecv.at[0], (w, near)).start()
+    remote(codes.at[4 * facing + 3], mid.at[0, 3], csend.at[1], msem.at[0, 3], up).start()
+    remote(codes.at[4 * cross + 3], mid.at[1, 3], csend.at[1], msem.at[1, 3], down).start()
+    remote(codes.at[pl.ds(4 * near + 3, 1)], codes4.at[n, 3:4], csend.at[1], crecv.at[1], (w, near)).start()
     own_codes = pltpu.make_async_copy(codes.at[pl.ds(4 * n, 4)], codes4.at[n], lsem.at[0])
     own_codes.start()
 
@@ -138,16 +142,15 @@
     remote(mid.at[0, 2], codes4.at[2 * down_half + core, 2], relays.at[0], crecv.at[0], up).start()
     pltpu.make_async_copy(mid.at[1, 2], mid.at[1, 2], msem.at[1, 2]).wait()
     remote(mid.at[1, 2], codes4.at[2 * up_half + core, 2], relays.at[0], crecv.at[0], down_other).start()
+
     pltpu.make_async_copy(send1, recv1.at[:, 1 - core], rsem1).wait()
     forward = remote(recv1.at[:, 1 - core], recv1.at[:, 1 - core], fsem1, gsem1, twin)
     forward.start()
-    remote(codes.at[4 * facing + 3], mid.at[0, 3], csend.at[1], msem.at[0, 3], up).start()
-    remote(codes.at[4 * cross + 3], mid.at[1, 3], csend.at[1], msem.at[1, 3], down).start()
-    remote(codes.at[pl.ds(4 * near + 3, 1)], codes4.at[n, 3:4], csend.at[1], crecv.at[1], (w, near)).start()
     pltpu.make_async_copy(send1, recv1.at[:, core], gsem1).wait()
+    columns = jnp.concatenate([recv1[:, :, :, f].reshape(1024, 128) for f in range(3)], axis=1)
+    mixed = mm(xrows[core], columns)
     for f in range(3):
-        mixed = mm(xrows[core], recv1[:, :, :, f].reshape(1024, 128))
-        send2[:, f] = mixed.reshape(128, 4, 128).astype(BF)
+        send2[:, f] = mixed[:, 128 * f : 128 * f + 128].reshape(128, 4, 128).astype(BF)
 
     def start2(i, c):
         to = lax.rem(chip + 1 + i, 128)
@@ -161,7 +164,6 @@
     remote(mid.at[0, 3], codes4.at[2 * down_half + core, 3], relays.at[0], crecv.at[1], up).start()
     pltpu.make_async_copy(mid.at[1, 3], mid.at[1, 3], msem.at[1, 3]).wait()
     remote(mid.at[1, 3], codes4.at[2 * up_half + core, 3], relays.at[0], crecv.at[1], down_other).start()
-
     for s in range(2):
 
         def flip(i, c):
@@ -191,11 +193,11 @@
         q = mm(misfit, dv[:, pl.ds(pl.multiple_of(384 * m, 384), 384)]).astype(BF)
         qsend[m] = q
         if d == 2:
-            remote(qsend.at[m, 0:128], midq.at[0, 0:128], qssem.at[0], msem.at[0, 4], up).start()
+            remote(qsend.at[m, 0:160], midq.at[0, 0:160], qssem.at[0], msem.at[0, 4], up).start()
         elif d == 3:
-            remote(qsend.at[m, 0:128], midq.at[1, 0:128], qssem.at[0], msem.at[1, 4], down).start()
+            remote(qsend.at[m, 0:160], midq.at[1, 0:160], qssem.at[0], msem.at[1, 4], down).start()
         elif d == 1:
-            remote(qsend.at[m, 0:128], qrecv.at[n, 0:128], qssem.at[0], qrsem.at[0], (w, m)).start()
+            remote(qsend.at[m, 0:160], qrecv.at[n, 0:160], qssem.at[0], qrsem.at[0], (w, m)).start()
     for m in range(4):
         old = codes4[m].reshape(288, 384).astype(F32)
         fresh[m] = shrink(old, tn(de[...], qsend[m]))
@@ -204,9 +206,11 @@
     for m in range(4):
         atoms[:, 384 * m : 384 * m + 384] = mm(de[...], fresh[m]).astype(BF)
     for h in range(2):
-        for b in range(4):
-            block = nt(atoms[...], dv[512 * h + 128 * b : 512 * h + 128 * b + 128, :])
-            send3[:, 2 * b + h] = block.reshape(16, 3, 4, 128).astype(BF)
+        for b in (0, 2):
+            block = nt(atoms[...], dv[512 * h + 128 * b : 512 * h + 128 * b + 256, :])
+            for k in range(2):
+                part = block[:, 128 * k : 128 * k + 128]
+                send3[:, 2 * (b + k) + h] = part.reshape(16, 3, 4, 128).astype(BF)
 
     def start3(i, c):
         to = lax.rem(chip + 1 + i, 128)
@@ -218,25 +222,31 @@
     lax.fori_loop(0, 127, start3, 0)
     own3 = pltpu.make_async_copy(send3.at[chip // 8, lax.rem(chip, 8)], recv3.at[core, chip], lsem.at[3])
     own3.start()
-    pltpu.make_async_copy(midq.at[0, 0:128], midq.at[0, 0:128], msem.at[0, 4]).wait()
-    remote(midq.at[0, 0:128], qrecv.at[2 * down_half + core, 0:128], relays.at[1], qrsem.at[0], up).start()
-    pltpu.make_async_copy(midq.at[1, 0:128], midq.at[1, 0:128], msem.at[1, 4]).wait()
-    remote(midq.at[1, 0:128], qrecv.at[2 * up_half + core, 0:128], relays.at[1], qrsem.at[0], down_other).start()
+    pltpu.make_async_copy(midq.at[0, 0:160], midq.at[0, 0:160], msem.at[0, 4]).wait()
+    remote(midq.at[0, 0:160], qrecv.at[2 * down_half + core, 0:160], relays.at[1], qrsem.at[0], up).start()
+    pltpu.make_async_copy(midq.at[1, 0:160], midq.at[1, 0:160], msem.at[1, 4]).wait()
+    remote(midq.at[1, 0:160], qrecv.at[2 * up_half + core, 0:160], relays.at[1], qrsem.at[0], down_other).start()
     pltpu.make_async_copy(send2.at[0:127], recv3.at[core, 0:127], rsem3).wait()
     own3.wait()
     forward3 = remote(recv3.at[core], recv3.at[core], fsem3, gsem3, twin)
     forward3.start()
-    remote(qsend.at[facing, 128:160], midq.at[0, 128:160], qssem.at[1], msem.at[0, 5], up).start()
-    remote(qsend.at[cross, 128:160], midq.at[1, 128:160], qssem.at[1], msem.at[1, 5], down).start()
-    remote(qsend.at[facing, 160:192], midq.at[0, 160:192], qssem.at[1], msem.at[0, 6], up).start()
-    remote(qsend.at[cross, 160:192], midq.at[1, 160:192], qssem.at[1], msem.at[1, 6], down).start()
-    remote(qsend.at[near, 128:192], qrecv.at[n, 128:192], qssem.at[1], qrsem.at[1], (w, near)).start()
+    remote(qsend.at[facing, 160:176], midq.at[0, 160:176], qssem.at[1], msem.at[0, 5], up).start()
+    remote(qsend.at[cross, 160:176], midq.at[1, 160:176], qssem.at[1], msem.at[1, 5], down).start()
+    remote(qsend.at[facing, 176:192], midq.at[0, 176:192], qssem.at[1], msem.at[0, 6], up).start()
+    remote(qsend.at[cross, 176:192], midq.at[1, 176:192], qssem.at[1], msem.at[1, 6], down).start()
+    remote(qsend.at[near, 160:192], qrecv.at[n, 160:192], qssem.at[1], qrsem.at[1], (w, near)).start()
     pltpu.make_async_copy(send2, recv3.at[1 - core], gsem3).wait()
 
+    back = sum(
+        mm(
+            xcols[k, :, 1 - core].reshape(512, 512),
+            jnp.concatenate([recv3[k, :, f].reshape(512, 128) for f in range(3)], axis=1),
+        )
+        for k in range(2)
+    )
     for f in range(3):
-        back = mm(xcols[0, :, 1 - core].reshape(512, 512), recv3[0, :, f].reshape(512, 128))
-        back += mm(xcols[1, :, 1 - core].reshape(512, 512), recv3[1, :, f].reshape(512, 128))
-        send4[:, :, f] = jnp.maximum(back, 0.0).reshape(16, 2, 16, 128).astype(BF)
+        part = jnp.maximum(back[:, 128 * f : 128 * f + 128], 0.0)
+        send4[:, :, f] = part.reshape(16, 2, 16, 128).astype(BF)
 
     def start4(i, c):
         a = lax.rem(w // 4 + i // 2, 16)
@@ -246,17 +256,17 @@
         return c
 
     lax.fori_loop(0, 32, start4, 0)
-    pltpu.make_async_copy(midq.at[0, 128:160], midq.at[0, 128:160], msem.at[0, 5]).wait()
-    remote(midq.at[0, 128:160], qrecv.at[2 * down_half + core, 128:160], relays.at[1], qrsem.at[1], up).start()
-    pltpu.make_async_copy(midq.at[1, 128:160], midq.at[1, 128:160], msem.at[1, 5]).wait()
-    remote(midq.at[1, 128:160], qrecv.at[2 * up_half + core, 128:160], relays.at[1], qrsem.at[1], down_other).start()
-    pltpu.make_async_copy(midq.at[0, 160:192], midq.at[0, 160:192], msem.at[0, 6]).wait()
-    remote(midq.at[0, 160:192], qrecv.at[2 * down_half + core, 160:192], relays.at[1], qrsem.at[1], up).start()
-    pltpu.make_async_copy(midq.at[1, 160:192], midq.at[1, 160:192], msem.at[1, 6]).wait()
-    remote(midq.at[1, 160:192], qrecv.at[2 * up_half + core, 160:192], relays.at[1], qrsem.at[1], down_other).start()
-
-    pltpu.make_async_copy(qsend.at[0:3, 0:128], qrecv.at[0:3, 0:128], qrsem.at[0]).wait()
-    pltpu.make_async_copy(qsend.at[0:3, 128:192], qrecv.at[0:3, 128:192], qrsem.at[1]).wait()
+    pltpu.make_async_copy(midq.at[0, 160:176], midq.at[0, 160:176], msem.at[0, 5]).wait()
+    remote(midq.at[0, 160:176], qrecv.at[2 * down_half + core, 160:176], relays.at[1], qrsem.at[1], up).start()
+    pltpu.make_async_copy(midq.at[1, 160:176], midq.at[1, 160:176], msem.at[1, 5]).wait()
+    remote(midq.at[1, 160:176], qrecv.at[2 * up_half + core, 160:176], relays.at[1], qrsem.at[1], down_other).start()
+    pltpu.make_async_copy(midq.at[0, 176:192], midq.at[0, 176:192], msem.at[0, 6]).wait()
+    remote(midq.at[0, 176:192], qrecv.at[2 * down_half + core, 176:192], relays.at[1], qrsem.at[1], up).start()
+    pltpu.make_async_copy(midq.at[1, 176:192], midq.at[1, 176:192], msem.at[1, 6]).wait()
+    remote(midq.at[1, 176:192], qrecv.at[2 * up_half + core, 176:192], relays.at[1], qrsem.at[1], down_other).start()
+
+    pltpu.make_async_copy(qsend.at[0:3, 0:160], qrecv.at[0:3, 0:160], qrsem.at[0]).wait()
+    pltpu.make_async_copy(qsend.at[0:3, 160:192], qrecv.at[0:3, 160:192], qrsem.at[1]).wait()
     load_codes.wait()
     own_q.wait()
     for m in range(4):
@@ -279,8 +289,8 @@
     pltpu.make_async_copy(send4, send4, ssem4).wait()
     pltpu.make_async_copy(codes4.at[0:3, 0:3], codes4.at[0:3, 0:3], csend.at[0]).wait()
     pltpu.make_async_copy(codes4.at[0:3, 3:4], codes4.at[0:3, 3:4], csend.at[1]).wait()
-    pltpu.make_async_copy(qsend.at[0:3, 0:128], qsend.at[0:3, 0:128], qssem.at[0]).wait()
-    pltpu.make_async_copy(qsend.at[0:3, 128:192], qsend.at[0:3, 128:192], qssem.at[1]).wait()
+    pltpu.make_async_copy(qsend.at[0:3, 0:160], qsend.at[0:3, 0:160], qssem.at[0]).wait()
+    pltpu.make_async_copy(qsend.at[0:3, 160:192], qsend.at[0:3, 160:192], qssem.at[1]).wait()
     pltpu.make_async_copy(mid, mid, relays.at[0]).wait()
     pltpu.make_async_copy(midq, midq, relays.at[1]).wait()
     put_low.wait()
@@ -349,9 +359,9 @@
             pltpu.VMEM((2, 192, 384), BF),
         ],
         compiler_params=pltpu.CompilerParams(
-            collective_id=0, has_side_effects=True, vmem_limit_bytes=54850000
+            collective_id=0, has_side_effects=True, vmem_limit_bytes=50331648
         ),
-    )(volume, codes_in, x_transform, y_atoms, de_atoms)
+    )(*(pltpu.with_memory_space_constraint(a, pltpu.HBM) for a in (volume, codes_in, x_transform, y_atoms, de_atoms)))
     return pl.pallas_call(
         finish,
         out_shape=(

time: 89.1 us -> 88.1 us (0.989)
  no operation moved by 1% of the time
where the time goes in v4:
time: 88.1 us; the launch traced here: 88 us
  Pallas kernels  87.3 us (99%)
    pallas_call x1, Pallas kernels, shards(): pl.pallas_call(kernel, out_shape=(jax.ShapeDtypeStruct((8, 72, 384), BF),...  86.1 us

profile of v4, /device:TPU:1, one launch (start us, length us, event | category | flops | bytes accessed | tf_op | source)
XLA Modules:
  0.0 88.0 jit_solution(15990728698699826522)
XLA Ops:
  0.6 86.1 %shard_map.68 = (bf16[8,72,384]{2,1,0:T(8,128)(2,1)S(1)}, bf16[8,72,384]{2,1,0:T(8,128)(2,1)S(1)}, bf16[16,2,3,16,128]{4,3,2,1,0:T(8,128)(2,1)S(1)}) custom-call(f32[16,48,256]{2,1,0:T(8,128)} %vol_in.1, bf16[16,72,384]{2,1,0:T(8,128)(2,1)} %codes.1, f32[1024,1024]{1,0:T(8,128)} %xin.1, bf16[1024,1536]{1,0:T(8,128)(2,1)} %din.1, bf16[48,72]{1,0:T(8,128)(2,1)} %de_in.1), custom_call_target="tpu_custom_call" | custom-call | tf_op jit(solution)/shard_map/pallas_call | solution.py:320
  86.7 1.3 %shard_map.69 = (bf16[16,72,384]{2,1,0:T(8,128)(2,1)}, bf16[16,48,256]{2,1,0:T(8,128)(2,1)}) custom-call(bf16[8,72,384]{2,1,0:T(8,128)(2,1)S(1)} %get-tuple-element.5.low, bf16[8,72,384]{2,1,0:T(8,128)(2,1)S(1)} %get-tuple-element.6.high, bf16[16,2,3,16,128]{4,3,2,1,0:T(8,128)(2,1)S(1)} %get-tuple-element.7.est), custom_call_target="tpu_custom_call" | custom-call | tf_op jit(solution)/shard_map/pallas_call | solution.py:365

commit v5 on v4

--- a/solution.py
+++ b/solution.py
@@ -205,21 +205,26 @@
     own_q.start()
     for m in range(4):
         atoms[:, 384 * m : 384 * m + 384] = mm(de[...], fresh[m]).astype(BF)
-    for h in range(2):
-        for b in (0, 2):
-            block = nt(atoms[...], dv[512 * h + 128 * b : 512 * h + 128 * b + 256, :])
-            for k in range(2):
-                part = block[:, 128 * k : 128 * k + 128]
-                send3[:, 2 * (b + k) + h] = part.reshape(16, 3, 4, 128).astype(BF)
-
-    def start3(i, c):
-        to = lax.rem(chip + 1 + i, 128)
-        remote(
-            send3.at[to // 8, lax.rem(to, 8)], recv3.at[core, chip], ssem3, rsem3, (to // 2, 2 * lax.rem(to, 2) + core)
-        ).start()
-        return c
-
-    lax.fori_loop(0, 127, start3, 0)
+    plane = 4 * half + low
+    for turn in range(4):
+        pair = lax.rem(plane // 2 + 1 + turn, 4)
+        block = nt(atoms[...], dv[pl.ds(pl.multiple_of(256 * pair, 256), 256), :])
+        for k in range(2):
+            part = block[:, 128 * k : 128 * k + 128]
+            send3[:, 4 * lax.rem(pair, 2) + 2 * k + pair // 2] = part.reshape(16, 3, 4, 128).astype(BF)
+
+        def start3(i, c):
+            t = lax.rem(w // 4 + 1 + i // 2, 16)
+            k = lax.rem(plane + 1 + i, 2)
+            b = 2 * lax.rem(pair, 2) + k
+            h = pair // 2
+            remote(
+                send3.at[t, 2 * b + h], recv3.at[core, chip], ssem3, rsem3, (4 * t + b, 2 * h + core)
+            ).start()
+            return c
+
+        lax.fori_loop(0, 32 if turn < 3 else 31, start3, 0)
+
     own3 = pltpu.make_async_copy(send3.at[chip // 8, lax.rem(chip, 8)], recv3.at[core, chip], lsem.at[3])
     own3.start()
     pltpu.make_async_copy(midq.at[0, 0:160], midq.at[0, 0:160], msem.at[0, 4]).wait()

time: 88.1 us -> 88 us (level)
  no operation moved by 1% of the time
where the time goes in v5:
time: 88 us; the launch traced here: 87.9 us
  Pallas kernels  87.3 us (99%)
    pallas_call x1, Pallas kernels, shards(): pl.pallas_call(kernel, out_shape=(jax.ShapeDtypeStruct((8, 72, 384), BF),...  86 us

profile of v5, /device:TPU:1, one launch (start us, length us, event | category | flops | bytes accessed | tf_op | source)
XLA Modules:
  0.0 87.9 jit_solution(1962277262249262396)
XLA Ops:
  0.6 86.0 %shard_map.68 = (bf16[8,72,384]{2,1,0:T(8,128)(2,1)S(1)}, bf16[8,72,384]{2,1,0:T(8,128)(2,1)S(1)}, bf16[16,2,3,16,128]{4,3,2,1,0:T(8,128)(2,1)S(1)}) custom-call(f32[16,48,256]{2,1,0:T(8,128)} %vol_in.1, bf16[16,72,384]{2,1,0:T(8,128)(2,1)} %codes.1, f32[1024,1024]{1,0:T(8,128)} %xin.1, bf16[1024,1536]{1,0:T(8,128)(2,1)} %din.1, bf16[48,72]{1,0:T(8,128)(2,1)} %de_in.1), custom_call_target="tpu_custom_call" | custom-call | tf_op jit(solution)/shard_map/pallas_call | solution.py:325
  86.7 1.3 %shard_map.69 = (bf16[16,72,384]{2,1,0:T(8,128)(2,1)}, bf16[16,48,256]{2,1,0:T(8,128)(2,1)}) custom-call(bf16[8,72,384]{2,1,0:T(8,128)(2,1)S(1)} %get-tuple-element.5.low, bf16[8,72,384]{2,1,0:T(8,128)(2,1)S(1)} %get-tuple-element.6.high, bf16[16,2,3,16,128]{4,3,2,1,0:T(8,128)(2,1)S(1)} %get-tuple-element.7.est), custom_call_target="tpu_custom_call" | custom-call | tf_op jit(solution)/shard_map/pallas_call | solution.py:370
